TPU v7x, 32 devices: a whole 2x2x4 slice. The times are simulated.
32 devices in a mesh: groups: 2 (over y), rows: 8 (over z, x), layers: 2 (over core).
Axes of the slice: x: 2, y: 2, z: 4, core: 2. Of those that a mesh axis runs over, the one named last changes fastest.
Arguments:
- train_grads: bfloat16 [6144, 2, 4096], P(('groups', 'rows'), 'layers'), parts along dimension 0, may hold values from -6 to 6
- query_grads: bfloat16 [2, 2048, 4096], P('layers', ('groups', 'rows')), parts along dimension 1, may hold values from -0.09375 to 0.09375
Outputs:
- scores: float32 [1024, 6144], P('layers', ('groups', 'rows')), parts along dimension 1
There are 2 independent parts, one for each index of `groups`. A program takes and returns all parts, laid end to end along the dimension named above; each array names one. Nothing has to cross between parts.
All inputs are finite; a program needn't handle non-finite values.
Results may differ from a plain program's by a relative error of at most 0.0003.
Values may be sent and summed in bfloat16 or wider, within the bound.
No kernel may reach another device: no remote copies, remote signals or barrier semaphores. Data moves between devices by JAX's collectives and lax.ppermute only.
A program may use at most 64 MiB of HBM per device.

v0:
```python
import jax
import jax.numpy as jnp
from jax import lax
from jax.sharding import PartitionSpec as P


def partial_scores(queries, train_grads):
    return jnp.einsum("lqk,nlk->qn", queries, train_grads, preferred_element_type=jnp.float32)


def shards(train_grads, query_grads):
    terms = partial_scores(lax.all_gather(query_grads, "rows", axis=1, tiled=True), train_grads)
    return lax.psum_scatter(terms, "layers", scatter_dimension=0, tiled=True)


def solution(mesh):
    in_specs = (P(("groups", "rows"), "layers", None), P("layers", ("groups", "rows"), None))
    out_specs = P("layers", ("groups", "rows"))
    return jax.shard_map(shards, mesh=mesh, in_specs=in_specs, out_specs=out_specs, check_vma=False)
```

profile of v0, /device:TPU:0, one launch (start us, length us, event | category | flops | bytes accessed | tf_op | source)
XLA Modules:
  0.0 159.1 jit_solution(11661200120718518420)
XLA Ops:
  6.5 0.0 copy-start
  6.5 0.0 all-gather.2.cloned.1.call-start
  6.5 0.7 all-gather.2.cloned.1.call-update
  7.3 0.0 reduce-scatter.2.cloned.1.call-start
  7.3 129.4 %all-gather.2.cloned.1.call-done = bf16[1,1024,4096]{2,1,0:T(8,128)(2,1)} async-done(((bf16[1,128,4096]{2,1,0:T(8,128)(2,1)}), bf16[1,1024,4096]{2,1,0:T(8,128)(2,1)}) %all-gather.2.cloned.1.call-update) | async-done | bytes 8388624 | tf_op jit(solution)/shard_map/all_gather | solution.py:12
  136.7 0.0 copy-done
  136.7 8.1 %fusion = f32[1024,384]{1,0:T(8,128)} fusion(bf16[1,1024,4096]{2,1,0:T(8,128)(2,1)} %all-gather.2.cloned.1.call-done, bf16[384,1,4096]{2,0,1:T(8,128)(2,1)S(1)} %copy-done), kind=kOutput, calls=%fused_computation | convolution fusion | flops 3221225472 | bytes 13107200 | tf_op jit(solution)/shard_map/lqk,nlk->qn/dot_general | solution.py:8
  144.8 0.0 reduce-scatter.2.cloned.1.call-update
  144.8 7.4 %reduce-scatter.2.cloned.1.call-done = f32[512,384]{1,0:T(8,128)} async-done(((f32[1024,384]{1,0:T(8,128)}), f32[512,384]{1,0:T(8,128)}) %reduce-scatter.2.cloned.1.call-update) | async-done | bytes 786448 | tf_op jit(solution)/shard_map/reduce_scatter | solution.py:13
Async XLA Ops:
  6.5 130.2 %copy-start = (bf16[384,1,4096]{2,0,1:T(8,128)(2,1)S(1)}, bf16[384,1,4096]{2,0,1:T(8,128)(2,1)}, u32[]{:S(2)}) copy-start(bf16[384,1,4096]{2,0,1:T(8,128)(2,1)} %param.2) | copy-start | bytes 9437188
  6.5 130.1 %all-gather.2.cloned.1.call-start = ((), (), s32[]{:S(2)}) async-start(), calls=%async_computation.1 | async-start | bytes 9437184 | tf_op jit(solution)/shard_map/all_gather | solution.py:12
  7.3 145.0 %reduce-scatter.2.cloned.1.call-start = ((), (), s32[]{:S(2)}) async-start(), calls=%async_computation.2 | async-start | bytes 2359296 | tf_op jit(solution)/shard_map/reduce_scatter | solution.py:13
Sparse Core Ops, SparseCore 0:
  9.5 127.1 all-gather.1
  145.0 7.2 reduce-scatter.1
where the time goes:
time: 159 us
  waiting for transfers between devices  137 us (86%)
  between operations  13.4 us (8%)
  matrix products  8.13 us (5%)
    all_gather x1, waiting for transfers between devices, shards(): lax.all_gather(query_grads, 'rows', axis=1, tiled=True)  129 us
    dot_general x1, matrix products, partial_scores(): jnp.einsum('lqk,nlk->qn', queries, train_grads, preferred_element_type=jn...  8.13 us
    reduce_scatter x1, waiting for transfers between devices, shards(): return lax.psum_scatter(terms, 'layers', scatter_dimension=0, tiled=True)  7.37 us
  transfers between devices with their start and end apart: 2, of which 2 were waited for; matrix products, arithmetic and copies ran while one was open for 0% of the time, Pallas kernels for 0%

commit v1 on v0

--- a/solution.py
+++ b/solution.py
@@ -9,7 +9,12 @@
 
 
 def shards(train_grads, query_grads):
-    terms = partial_scores(lax.all_gather(query_grads, "rows", axis=1, tiled=True), train_grads)
+    terms = partial_scores(
+        jnp.concatenate(
+            lax.all_to_all(jnp.stack([query_grads] * lax.axis_size("rows")), "rows", 0, 0), axis=1
+        ),
+        train_grads,
+    )
     return lax.psum_scatter(terms, "layers", scatter_dimension=0, tiled=True)
 
 

time: 159 us -> 220 us (1.38)
  blocking collectives: 0 us -> 190 us
  waiting for transfers between devices: 137 us -> 8.26 us
  matrix products: 8.13 us -> 5.67 us
  local copies, waits for them, and re-layouts: 0.01 us -> 2.42 us
    all_to_all x0 -> x1, blocking collectives: none -> 190 us  [shards(): lax.all_to_all(jnp.stack([query_grads] * lax.axis_size('rows')), 'rows',...]
    all_gather x1 -> x0, waiting for transfers between devices: 129 us -> none  [shards(): lax.all_gather(query_grads, 'rows', axis=1, tiled=True)]
    dot_general x1, matrix products: 8.13 us -> 5.67 us  [partial_scores(): jnp.einsum('lqk,nlk->qn', queries, train_grads, preferred_element_type=jn...]
    another operation x0 -> x1, local copies, waits for them, and re-layouts: none -> 2.41 us  [shards(): jnp.stack([query_grads] * lax.axis_size('rows'))]
  transfers between devices with their start and end apart: 2 -> 1, of which waited for: 2 -> 1; matrix products, arithmetic and copies ran while one was open for 0% -> 0% of each run, Pallas kernels for 0% -> 0%
where the time goes in v1:
time: 220 us
  blocking collectives  190 us (86%)
  between operations  13.4 us (6%)
  waiting for transfers between devices  8.26 us (4%)
  matrix products  5.67 us (3%)
  local copies, waits for them, and re-layouts  2.42 us (1%)
    all_to_all x1, blocking collectives, shards(): lax.all_to_all(jnp.stack([query_grads] * lax.axis_size('rows')), 'rows',...  190 us
    reduce_scatter x1, waiting for transfers between devices, shards(): return lax.psum_scatter(terms, 'layers', scatter_dimension=0, tiled=True)  8.24 us
    dot_general x1, matrix products, partial_scores(): jnp.einsum('lqk,nlk->qn', queries, train_grads, preferred_element_type=jn...  5.67 us
  transfers between devices with their start and end apart: 1, of which 1 were waited for; matrix products, arithmetic and copies ran while one was open for 0% of the time, Pallas kernels for 0%

profile of v1, /device:TPU:0, one launch (start us, length us, event | category | flops | bytes accessed | tf_op | source)
XLA Modules:
  0.0 219.9 jit_solution(1547742733377846307)
XLA Ops:
  6.5 0.0 copy-start
  6.5 0.0 reduce-scatter.2.cloned.1.call-start
  6.5 2.4 %stack.2 = bf16[8,1,128,4096]{3,2,1,0:T(8,128)(2,1)S(1)} broadcast(bf16[128,4096]{1,0:T(8,128)(2,1)} %bitcast.7), dimensions={2,3} | broadcast | bytes 9437184 | tf_op jit(solution)/shard_map/stack | solution.py:14
  9.0 190.1 %all_to_all.5 = bf16[8,1,128,4096]{3,2,1,0:T(8,128)(2,1)S(1)} all-to-all(bf16[8,1,128,4096]{3,2,1,0:T(8,128)(2,1)S(1)} %stack.2), channel_id=1, replica_groups=mesh['groups'=2,'rows'=8,'layers'=2] {'rows'}, dimensions={0} | all-to-all | bytes 16777216 | tf_op jit(solution)/shard_map/all_to_all | solution.py:14
  199.1 0.0 copy-done
  199.1 5.7 %fusion = f32[1024,384]{1,0:T(8,128)} fusion(bf16[1024,4096]{1,0:T(8,128)(2,1)S(1)} %bitcast.6, bf16[384,1,4096]{2,0,1:T(8,128)(2,1)S(1)} %copy-done), kind=kOutput, calls=%fused_computation | convolution fusion | flops 3221225472 | bytes 13107200 | tf_op jit(solution)/shard_map/lqk,nlk->qn/dot_general | solution.py:8
  204.8 0.0 reduce-scatter.2.cloned.1.call-update
  204.8 8.2 %reduce-scatter.2.cloned.1.call-done = f32[512,384]{1,0:T(8,128)} async-done(((f32[1024,384]{1,0:T(8,128)}), f32[512,384]{1,0:T(8,128)}) %reduce-scatter.2.cloned.1.call-update) | async-done | bytes 786448 | tf_op jit(solution)/shard_map/reduce_scatter | solution.py:18
Async XLA Ops:
  6.5 192.6 %copy-start = (bf16[384,1,4096]{2,0,1:T(8,128)(2,1)S(1)}, bf16[384,1,4096]{2,0,1:T(8,128)(2,1)}, u32[]{:S(2)}) copy-start(bf16[384,1,4096]{2,0,1:T(8,128)(2,1)} %param.2) | copy-start | bytes 9437188
  6.5 206.5 %reduce-scatter.2.cloned.1.call-start = ((), (), s32[]{:S(2)}) async-start(), calls=%async_computation.2 | async-start | bytes 2359296 | tf_op jit(solution)/shard_map/reduce_scatter | solution.py:18
Sparse Core Ops, SparseCore 0:
  204.9 8.0 reduce-scatter.1
